TPU v7x, 32 devices: a whole 2x2x4 slice. The times are simulated.
32 devices in a mesh: req: 4 (over x, core), mlp: 8 (over z, y).
Axes of the slice: x: 2, y: 2, z: 4, core: 2. Of those that a mesh axis runs over, the one named last changes fastest.
Arguments:
- resid: bfloat16 [4096, 3072], P(('req', 'mlp')), may hold values from -6 to 6
- queries: bfloat16 [4096, 1536], P(('req', 'mlp')), may hold values from -240 to 240
- fresh_keys: bfloat16 [4096, 256], P(('req', 'mlp')), may hold values from -6 to 6
- fresh_values: bfloat16 [4096, 256], P(('req', 'mlp')), may hold values from -6 to 6
- paged_key_cache: bfloat16 [64, 128, 256], P(('req', 'mlp')), may hold values from -6 to 6
- paged_value_cache: bfloat16 [64, 128, 256], P(('req', 'mlp')), may hold values from -6 to 6
- page_table: int32 [4, 16], P('req'), may hold values from 0 to 15, as said below
- cache_lengths: int32 [4], P('req'), may hold values from 1 to 2048, as said below
- out_weight: bfloat16 [1536, 3072], replicated, may hold values from -0.15625 to 0.15625
- norm_gain: float32 [3072], replicated, may hold values from 0.5 to 1.5
- gate_weight: bfloat16 [3072, 8192], P('req', 'mlp'), may hold values from -0.109375 to 0.109375
- up_weight: bfloat16 [3072, 8192], P('req', 'mlp'), may hold values from -0.109375 to 0.109375
- down_weight: bfloat16 [8192, 3072], P('mlp', 'req'), may hold values from -0.0625 to 0.0625
Outputs:
- layer_out: bfloat16 [4096, 3072], P(('req', 'mlp'))
Inputs may be any that keep to these rules, and one draw needn't show every extreme that they name: `page_table`: within the 1 request of one index of req the entries are a permutation of 0 to 15. `cache_lengths`: half of the requests hold at most 128 cached tokens, the other half more than 1920; some request holds exactly 2048.
All inputs are finite; a program needn't handle non-finite values.
Results may differ from a plain program's by a relative error of at most 0.0085.
Values may be sent and summed in bfloat16 or wider, within the bound.
A program may use at most 128 MiB of HBM per device.

v0:
```python
import jax
import jax.numpy as jnp
from jax import lax
from jax.sharding import PartitionSpec as P

QUERY_HEADS = 12
KEY_VALUE_HEADS = 2
HEAD_SIZE = 128
REQ_DEV = 1


def body(
    resid,
    queries,
    fresh_keys,
    fresh_values,
    paged_key_cache,
    paged_value_cache,
    page_table,
    cache_lengths,
    out_weight,
    norm_gain,
    gate_weight,
    up_weight,
    down_weight,
):
    token_position = queries.shape[0]
    group_ratio = QUERY_HEADS // KEY_VALUE_HEADS
    scale = HEAD_SIZE ** (-0.5)
    seq_len = token_position * lax.axis_size("mlp") // REQ_DEV
    place = lax.axis_index("mlp")
    first = place * token_position
    request = first // seq_len
    length = lax.dynamic_index_in_dim(cache_lengths, request, 0, keepdims=False)
    table_row = lax.dynamic_index_in_dim(page_table, request, 0, keepdims=False)
    heads_of_queries = queries.reshape(token_position, KEY_VALUE_HEADS, group_ratio, HEAD_SIZE)

    def update(state, joined_keys, joined_values, valid):
        peak, total, summed = state
        heads_of_keys = joined_keys.reshape(-1, KEY_VALUE_HEADS, HEAD_SIZE)
        heads_of_values = joined_values.reshape(-1, KEY_VALUE_HEADS, HEAD_SIZE)
        scores = (
            jnp.einsum(
                "tgrd,kgd->grtk",
                heads_of_queries,
                heads_of_keys,
                preferred_element_type=jnp.float32,
            )
            * scale
        )
        scores = jnp.where(valid, scores, -1e30)
        new_peak = jnp.maximum(peak, jnp.max(scores, axis=-1))
        expo = jnp.where(valid, jnp.exp(scores - new_peak[..., None]), 0.0)
        factor = jnp.exp(peak - new_peak)
        total = total * factor + jnp.sum(expo, axis=-1)
        summed = summed * factor[..., None] + jnp.einsum(
            "grtk,kgd->grtd",
            expo.astype(jnp.bfloat16),
            heads_of_values,
            preferred_element_type=jnp.float32,
        )
        return (new_peak, total, summed)

    state = (
        jnp.full((KEY_VALUE_HEADS, group_ratio, token_position), -1e30, jnp.float32),
        jnp.zeros((KEY_VALUE_HEADS, group_ratio, token_position), jnp.float32),
        jnp.zeros((KEY_VALUE_HEADS, group_ratio, token_position, HEAD_SIZE), jnp.float32),
    )
    rows_of_queries = first + jnp.arange(token_position, dtype=jnp.int32)
    rows_of_keys = lax.all_gather(fresh_keys, "mlp", axis=0, tiled=True)
    rows_of_values = lax.all_gather(fresh_values, "mlp", axis=0, tiled=True)
    count = rows_of_keys.shape[0]
    key_index = jnp.arange(count, dtype=jnp.int32)
    same = key_index[None, :] // seq_len == rows_of_queries[:, None] // seq_len
    valid = same & (key_index[None, :] <= rows_of_queries[:, None])
    state = update(state, rows_of_keys, rows_of_values, valid)
    key_page = lax.all_gather(paged_key_cache, "mlp", axis=0, tiled=True)
    value_page = lax.all_gather(paged_value_cache, "mlp", axis=0, tiled=True)
    count = key_page.shape[0]
    depth = key_page.shape[1]
    cache_positions = jnp.arange(count, dtype=jnp.int32)
    match = table_row[None, :] == cache_positions[:, None]
    owned = jnp.any(match, axis=1)
    page = jnp.sum(
        jnp.where(match, jnp.arange(table_row.shape[0], dtype=jnp.int32)[None, :], 0), axis=1
    )
    positions = page[:, None] * depth + jnp.arange(depth, dtype=jnp.int32)[None, :]
    live = (owned[:, None] & (positions < length)).reshape(1, count * depth)
    joined_keys = key_page.reshape(count * depth, -1)
    joined_values = value_page.reshape(count * depth, -1)
    state = update(state, joined_keys, joined_values, live)
    peak, total, summed = state
    attended = summed / total[..., None]
    attn = (
        jnp.transpose(attended, (2, 0, 1, 3))
        .reshape(token_position, QUERY_HEADS * HEAD_SIZE)
        .astype(jnp.bfloat16)
    )
    h = resid.astype(jnp.float32) + jnp.dot(attn, out_weight, preferred_element_type=jnp.float32)
    normed = (h * lax.rsqrt(jnp.mean(h * h, axis=-1, keepdims=True) + 1e-05) * norm_gain).astype(
        jnp.bfloat16
    )
    whole = lax.all_gather(normed, "mlp", axis=0, tiled=True)

    def add_rows(piece):
        return jnp.dot(whole, piece, preferred_element_type=jnp.float32)

    gate = add_rows(lax.all_gather(gate_weight, "req", axis=0, tiled=True))
    upper = add_rows(lax.all_gather(up_weight, "req", axis=0, tiled=True))
    hidden = (jax.nn.silu(gate) * upper).astype(jnp.bfloat16)
    terms = jnp.dot(
        hidden,
        lax.all_gather(down_weight, "req", axis=1, tiled=True),
        preferred_element_type=jnp.float32,
    )
    mixed = lax.psum_scatter(
        terms.astype(jnp.bfloat16), "mlp", scatter_dimension=0, tiled=True
    ).astype(jnp.float32)
    return (h + mixed).astype(jnp.bfloat16)


def solution(mesh):
    placed = (
        P(("req", "mlp"), None),
        P(("req", "mlp"), None),
        P(("req", "mlp"), None),
        P(("req", "mlp"), None),
        P(("req", "mlp"), None, None),
        P(("req", "mlp"), None, None),
        P("req", None),
        P("req"),
        P(),
        P(),
        P("req", "mlp"),
        P("req", "mlp"),
        P("mlp", "req"),
    )
    return jax.shard_map(
        body, mesh=mesh, in_specs=placed, out_specs=P(("req", "mlp"), None), check_vma=False
    )
```

profile of v0, /device:TPU:0, one launch (start us, length us, event | category | flops | bytes accessed | tf_op | source)
XLA Modules:
  0.0 476.9 jit_solution(3383910963019407040)
XLA Ops:
  6.5 0.0 all-gather.7.cloned.1.call-start
  6.5 0.7 all-gather.7.cloned.1.call-update
  7.3 0.0 all-gather.9.cloned.1.call-start
  7.3 0.7 all-gather.9.cloned.1.call-update
  8.0 0.0 all-gather.13.cloned.1.call-start
  8.1 0.7 all-gather.13.cloned.1.call-update
  8.7 0.0 all-gather.11.cloned.1.call-start
  9.4 1.2 copy.43
  10.7 1.0 copy.42
  11.6 34.4 %all_gather.25 = bf16[1024,256]{1,0:T(8,128)(2,1)S(1)} all-gather(bf16[128,256]{1,0:T(8,128)(2,1)} %param.16), channel_id=1, replica_groups=mesh['req'=4,'mlp'=8] {'mlp'}, dimensions={0}, use_global_device_ids=true | all-gather | bytes 589824 | tf_op jit(solution)/shard_map/all_gather | solution.py:71
  46.0 1.0 copy.46
  47.0 0.8 fusion.47
  47.8 0.8 select_reduce_fusion
  48.6 0.1 fusion.49
  48.7 0.2 fusion.42
  48.9 0.0 copy-start
  48.9 28.2 %all_gather.24 = bf16[1024,256]{0,1:T(8,128)(2,1)S(1)} all-gather(bf16[128,256]{0,1:T(8,128)(2,1)S(1)} %copy.42), channel_id=1, replica_groups=mesh['req'=4,'mlp'=8] {'mlp'}, dimensions={0}, use_global_device_ids=true | all-gather | bytes 589824 | tf_op jit(solution)/shard_map/all_gather | solution.py:70
  77.1 0.0 copy-done
  77.1 3.8 fusion.8
  80.9 0.0 all-gather.7.cloned.1.call-done
  80.9 1.4 reshape.148
  82.4 14.6 %all-gather.9.cloned.1.call-done = bf16[16,128,256]{2,1,0:T(8,128)(2,1)} async-done(((bf16[2,128,256]{2,1,0:T(8,128)(2,1)}), bf16[16,128,256]{2,1,0:T(8,128)(2,1)}) %all-gather.9.cloned.1.call-update) | async-done | bytes 1048592 | tf_op jit(solution)/shard_map/all_gather | solution.py:78
  97.0 0.0 slice-start
  97.0 2.4 reshape.149
  99.3 1.9 bitcast_reduce_fusion
  101.3 0.0 slice-done
  101.3 0.2 slice-done.1
  101.5 0.0 copy-done.1
  101.5 1.5 fusion.9
  103.0 0.0 copy-start.4
  103.1 3.8 fusion.2
  106.9 0.0 copy-done.4
  106.9 0.0 copy-start.2
  106.9 0.0 slice-start.2
  106.9 1.7 fusion.26
  108.6 0.0 copy-done.2
  108.6 0.0 slice-start.3
  108.6 0.0 slice-start.4
  108.6 0.0 copy-start.3
  108.6 3.4 fusion.37
  112.0 0.0 slice-done.2
  112.0 0.0 slice-done.3
  112.0 0.0 slice-done.4
  112.0 0.0 copy-done.3
  112.0 0.0 copy-start.5
  112.1 1.6 multiply_reduce_fusion
  113.6 0.0 copy-done.5
  113.6 1.1 multiply_convert_fusion.1
  114.8 0.0 all-gather.11.cloned.1.call-update
  114.8 0.0 all-gather.15.cloned.1.call-start
  114.8 0.5 all-gather.15.cloned.1.call-update
  115.4 0.0 all-gather.17.cloned.1.call-start
  115.4 0.5 all-gather.17.cloned.1.call-update
  115.9 0.0 reduce-scatter.2.cloned.1.call-start
  116.0 27.7 %all-gather.13.cloned.1.call-done = bf16[3072,1024]{1,0:T(8,128)(2,1)} async-done(((bf16[768,1024]{1,0:T(8,128)(2,1)}), bf16[3072,1024]{1,0:T(8,128)(2,1)}) %all-gather.13.cloned.1.call-update) | async-done | bytes 6291472 | tf_op jit(solution)/shard_map/all_gather | solution.py:108
  143.7 101.1 %all-gather.11.cloned.1.call-done = bf16[1024,3072]{1,0:T(8,128)(2,1)} async-done(((bf16[128,3072]{1,0:T(8,128)(2,1)}), bf16[1024,3072]{1,0:T(8,128)(2,1)}) %all-gather.11.cloned.1.call-update) | async-done | bytes 6291472 | tf_op jit(solution)/shard_map/all_gather | solution.py:103
  244.8 11.9 %fusion.61 = f32[1024,1024]{1,0:T(8,128)} fusion(bf16[1024,3072]{1,0:T(8,128)(2,1)} %all-gather.11.cloned.1.call-done, bf16[3072,1024]{1,0:T(8,128)(2,1)} %all-gather.13.cloned.1.call-done), kind=kOutput, calls=%fused_computation.71 | convolution fusion | flops 6442450944 | bytes 16777216 | tf_op jit(solution)/shard_map/dot_general | solution.py:106
  256.8 34.1 %all-gather.15.cloned.1.call-done = bf16[3072,1024]{1,0:T(8,128)(2,1)} async-done(((bf16[768,1024]{1,0:T(8,128)(2,1)}), bf16[3072,1024]{1,0:T(8,128)(2,1)}) %all-gather.15.cloned.1.call-update) | async-done | bytes 6291472 | tf_op jit(solution)/shard_map/all_gather | solution.py:109
  290.8 12.7 %multiply_convert_fusion = bf16[1024,1024]{1,0:T(8,128)(2,1)} fusion(f32[1024,1024]{1,0:T(8,128)} %fusion.61, bf16[1024,3072]{1,0:T(8,128)(2,1)} %all-gather.11.cloned.1.call-done, bf16[3072,1024]{1,0:T(8,128)(2,1)} %all-gather.15.cloned.1.call-done), kind=kOutput, calls=%fused_computation.16 | convolution fusion | flops 6448742400 | bytes 18874368 | tf_op jit(solution)/shard_map/dot_general | solution.py:106
  303.5 35.1 %all-gather.17.cloned.1.call-done = bf16[1024,3072]{1,0:T(8,128)(2,1)} async-done(((bf16[1024,768]{1,0:T(8,128)(2,1)}), bf16[1024,3072]{1,0:T(8,128)(2,1)}) %all-gather.17.cloned.1.call-update) | async-done | bytes 6291472 | tf_op jit(solution)/shard_map/all_gather | solution.py:113
  338.7 11.1 %convolution_convert_fusion = bf16[1024,3072]{1,0:T(8,128)(2,1)} fusion(bf16[1024,1024]{1,0:T(8,128)(2,1)} %multiply_convert_fusion, bf16[1024,3072]{1,0:T(8,128)(2,1)} %all-gather.17.cloned.1.call-done), kind=kOutput, calls=%fused_computation.12 | convolution fusion | flops 6445596672 | bytes 14680064 | tf_op jit(solution)/shard_map/dot_general | solution.py:111
  349.8 0.0 reduce-scatter.2.cloned.1.call-update
  349.8 118.1 %reduce-scatter.2.cloned.1.call-done = bf16[128,3072]{1,0:T(8,128)(2,1)} async-done(((bf16[1024,3072]{1,0:T(8,128)(2,1)}), bf16[128,3072]{1,0:T(8,128)(2,1)}) %reduce-scatter.2.cloned.1.call-update) | async-done | bytes 786448 | tf_op jit(solution)/shard_map/reduce_scatter | solution.py:116
  467.8 2.2 add_convert_fusion
  (10 shorter events, 0.1 us)
Async XLA Ops:
  6.5 74.4 %all-gather.7.cloned.1.call-start = ((), (), s32[]{:S(2)}) async-start(), calls=%async_computation.1 | async-start | bytes 1179648 | tf_op jit(solution)/shard_map/all_gather | solution.py:77
  7.3 89.7 %all-gather.9.cloned.1.call-start = ((), (), s32[]{:S(2)}) async-start(), calls=%async_computation.2 | async-start | bytes 1179648 | tf_op jit(solution)/shard_map/all_gather | solution.py:78
  8.0 135.7 %all-gather.13.cloned.1.call-start = ((), (), s32[]{:S(2)}) async-start(), calls=%async_computation.4 | async-start | bytes 7864320 | tf_op jit(solution)/shard_map/all_gather | solution.py:108
  8.7 236.1 %all-gather.11.cloned.1.call-start = ((), (), s32[]{:S(2)}) async-start(), calls=%async_computation.3 | async-start | bytes 7077888 | tf_op jit(solution)/shard_map/all_gather | solution.py:103
  48.9 28.2 %copy-start = (pred[128,1024]{0,1:T(8,128)(4,1)}, pred[128,1024]{0,1:T(8,128)(4,1)S(1)}, u32[]{:S(2)}) copy-start(pred[128,1024]{0,1:T(8,128)(4,1)S(1)} %fusion.42) | copy-start | bytes 393220
  97.0 4.3 slice-start
  99.3 2.2 slice-start.1
  99.3 2.2 copy-start.1
  103.0 3.8 copy-start.4
  106.9 1.7 copy-start.2
  106.9 5.1 %slice-start.2 = ((s8[9437184]{0:T(1024)(128)(4,1)}), s8[4194304]{0:T(1024)(128)(4,1)S(1)}, s32[]{:S(2)}) async-start(s8[9437184]{0:T(1024)(128)(4,1)} %bitcast.105), calls=%async_computation.10 | async-start | bytes 8388608
  108.6 3.4 slice-start.3
  108.6 3.4 slice-start.4
  108.6 3.4 copy-start.3
  112.0 1.6 copy-start.5
  114.8 176.0 %all-gather.15.cloned.1.call-start = ((), (), s32[]{:S(2)}) async-start(), calls=%async_computation.5 | async-start | bytes 7864320 | tf_op jit(solution)/shard_map/all_gather | solution.py:109
  115.4 223.3 %all-gather.17.cloned.1.call-start = ((), (), s32[]{:S(2)}) async-start(), calls=%async_computation.6 | async-start | bytes 7864320 | tf_op jit(solution)/shard_map/all_gather | solution.py:113
  115.9 351.9 %reduce-scatter.2.cloned.1.call-start = ((), (), s32[]{:S(2)}) async-start(), calls=%async_computation.7 | async-start | bytes 7077888 | tf_op jit(solution)/shard_map/reduce_scatter | solution.py:116
Sparse Core Ops, SparseCore 0:
  9.5 44.9 all-gather.6
  56.6 40.3 all-gather.8
  98.5 45.1 all-gather.12
  145.7 99.0 all-gather.10
  246.2 44.5 all-gather.14
  292.2 46.3 all-gather.16
  349.9 117.9 reduce-scatter.1
where the time goes:
time: 477 us
  waiting for transfers between devices  334 us (70%)
  blocking collectives  62.6 us (13%)
  matrix products  48.1 us (10%)
  between operations  14.4 us (3%)
  other arithmetic  10.4 us (2%)
  local copies, waits for them, and re-layouts  7.24 us (2%)
    reduce_scatter x1, waiting for transfers between devices, body(): lax.psum_scatter(terms.astype(jnp.bfloat16), 'mlp', scatter_dimension=0,...  118 us
    all_gather x1, waiting for transfers between devices, body(): whole = lax.all_gather(normed, 'mlp', axis=0, tiled=True)  101 us
    all_gather x1, waiting for transfers between devices, body(): lax.all_gather(down_weight, 'req', axis=1, tiled=True)  35.1 us
    all_gather x1, blocking collectives, body(): rows_of_values = lax.all_gather(fresh_values, 'mlp', axis=0, tiled=True)  34.4 us
    all_gather x1, waiting for transfers between devices, body(): upper = add_rows(lax.all_gather(up_weight, 'req', axis=0, tiled=True))  34.1 us
    all_gather x1, blocking collectives, body(): rows_of_keys = lax.all_gather(fresh_keys, 'mlp', axis=0, tiled=True)  28.2 us
    all_gather x1, waiting for transfers between devices, body(): gate = add_rows(lax.all_gather(gate_weight, 'req', axis=0, tiled=True))  27.7 us
    dot_general x2, matrix products, add_rows(): return jnp.dot(whole, piece, preferred_element_type=jnp.float32)  24.7 us
  transfers between devices with their start and end apart: 7, of which 6 were waited for; matrix products, arithmetic and copies ran while one was open for 11% of the time, Pallas kernels for 0%

commit v1 on v0

--- a/solution.py
+++ b/solution.py
@@ -7,6 +7,19 @@
 KEY_VALUE_HEADS = 2
 HEAD_SIZE = 128
 REQ_DEV = 1
+
+
+def ring_gather(x, axis, dim):
+    ways = lax.axis_size(axis)
+    up = [(d, (d + 1) % ways) for d in range(ways)]
+    down = [(d, (d - 1) % ways) for d in range(ways)]
+    earlier, later = ([x], [x])
+    for _ in range(ways // 2):
+        earlier.append(lax.ppermute(earlier[-1], axis, up))
+    for _ in range((ways - 1) // 2):
+        later.append(lax.ppermute(later[-1], axis, down))
+    line = jnp.concatenate([*earlier[::-1], *later[1:]], axis=dim)
+    return jnp.roll(line, (lax.axis_index(axis) - ways // 2) * x.shape[dim], axis=dim)
 
 
 def body(
@@ -106,7 +119,7 @@
         return jnp.dot(whole, piece, preferred_element_type=jnp.float32)
 
     gate = add_rows(lax.all_gather(gate_weight, "req", axis=0, tiled=True))
-    upper = add_rows(lax.all_gather(up_weight, "req", axis=0, tiled=True))
+    upper = add_rows(ring_gather(up_weight, "req", 0))
     hidden = (jax.nn.silu(gate) * upper).astype(jnp.bfloat16)
     terms = jnp.dot(
         hidden,

time: 477 us -> 442 us (0.927)
  waiting for transfers between devices: 334 us -> 281 us
  local copies, waits for them, and re-layouts: 7.24 us -> 25.9 us
    ppermute x0 -> x3, waiting for transfers between devices: none -> 78.4 us  [the longest x2 78.4 us: ring_gather(): earlier.append(lax.ppermute(earlier[-1], axis, up))]
    all_gather x1, waiting for transfers between devices: 101 us -> 43 us  [body(): whole = lax.all_gather(normed, 'mlp', axis=0, tiled=True)]
    all_gather x1 -> x0, waiting for transfers between devices: 34.1 us -> none  [body(): upper = add_rows(lax.all_gather(up_weight, 'req', axis=0, tiled=True))]
    all_gather x1, waiting for transfers between devices: 27.7 us -> 0.01 us  [body(): gate = add_rows(lax.all_gather(gate_weight, 'req', axis=0, tiled=True))]
    unnamed x24 -> x35, local copies, waits for them, and re-layouts: 2.44 us -> 18.5 us
    all_gather x1, waiting for transfers between devices: 35.1 us -> 24.4 us  [body(): lax.all_gather(down_weight, 'req', axis=1, tiled=True)]
  transfers between devices with their start and end apart: 7 -> 9, of which waited for: 6 -> 6; matrix products, arithmetic and copies ran while one was open for 11% -> 15% of each run, Pallas kernels for 0% -> 0%
where the time goes in v1:
time: 442 us; the launch traced here: 441 us
  waiting for transfers between devices  281 us (64%)
  blocking collectives  62.5 us (14%)
  matrix products  45.2 us (10%)
  local copies, waits for them, and re-layouts  25.9 us (6%)
  between operations  14.4 us (3%)
  other arithmetic  10.4 us (2%)
    reduce_scatter x1, waiting for transfers between devices, body(): lax.psum_scatter(terms.astype(jnp.bfloat16), 'mlp', scatter_dimension=0,...  118 us
    ppermute x2, waiting for transfers between devices, ring_gather(): earlier.append(lax.ppermute(earlier[-1], axis, up))  78.4 us
    all_gather x1, waiting for transfers between devices, body(): whole = lax.all_gather(normed, 'mlp', axis=0, tiled=True)  43 us
    all_gather x1, blocking collectives, body(): rows_of_values = lax.all_gather(fresh_values, 'mlp', axis=0, tiled=True)  34.4 us
    all_gather x1, blocking collectives, body(): rows_of_keys = lax.all_gather(fresh_keys, 'mlp', axis=0, tiled=True)  28.1 us
    all_gather x1, waiting for transfers between devices, body(): lax.all_gather(down_weight, 'req', axis=1, tiled=True)  24.4 us
    dot_general x2, matrix products, add_rows(): return jnp.dot(whole, piece, preferred_element_type=jnp.float32)  21.6 us
    unnamed x35, local copies, waits for them, and re-layouts  18.5 us
  transfers between devices with their start and end apart: 9, of which 6 were waited for; matrix products, arithmetic and copies ran while one was open for 15% of the time, Pallas kernels for 0%

profile of v1, /device:TPU:0, one launch (start us, length us, event | category | flops | bytes accessed | tf_op | source)
XLA Modules:
  0.0 441.2 jit_solution(1855884260099141964)
XLA Ops:
  6.5 0.0 all-gather.6.cloned.1.call-start
  6.5 0.7 all-gather.6.cloned.1.call-update
  7.3 0.0 all-gather.8.cloned.1.call-start
  7.3 0.7 all-gather.8.cloned.1.call-update
  8.0 0.0 all-gather.12.cloned.1.call-start
  8.1 0.7 all-gather.12.cloned.1.call-update
  8.7 0.0 all-gather.10.cloned.1.call-start
  8.8 1.2 copy.43
  10.0 1.0 copy.42
  11.6 34.4 %all_gather.22 = bf16[1024,256]{1,0:T(8,128)(2,1)S(1)} all-gather(bf16[128,256]{1,0:T(8,128)(2,1)} %param.16), channel_id=1, replica_groups=mesh['req'=4,'mlp'=8] {'mlp'}, dimensions={0}, use_global_device_ids=true | all-gather | bytes 589824 | tf_op jit(solution)/shard_map/all_gather | solution.py:84
  46.0 1.0 copy.46
  47.0 0.8 fusion.51
  47.8 0.8 select_reduce_fusion
  48.6 0.1 fusion.53
  48.7 0.2 fusion.46
  48.9 28.1 %all_gather.21 = bf16[1024,256]{0,1:T(8,128)(2,1)S(1)} all-gather(bf16[128,256]{0,1:T(8,128)(2,1)S(1)} %copy.42), channel_id=1, replica_groups=mesh['req'=4,'mlp'=8] {'mlp'}, dimensions={0}, use_global_device_ids=true | all-gather | bytes 589824 | tf_op jit(solution)/shard_map/all_gather | solution.py:83
  77.0 0.0 copy-done.1
  77.0 3.8 fusion.10
  80.8 1.3 reshape.148
  82.1 14.2 %all-gather.8.cloned.1.call-done = bf16[16,128,256]{2,1,0:T(8,128)(2,1)} async-done(((bf16[2,128,256]{2,1,0:T(8,128)(2,1)}), bf16[16,128,256]{2,1,0:T(8,128)(2,1)}) %all-gather.8.cloned.1.call-update) | async-done | bytes 1048592 | tf_op jit(solution)/shard_map/all_gather | solution.py:91
  96.3 2.4 reshape.149
  98.7 1.9 bitcast_reduce_fusion
  100.7 0.2 slice-done.1
  100.9 0.0 copy-done.2
  100.9 1.5 fusion.11
  102.4 0.0 copy-start.5
  102.4 3.8 fusion.2
  106.2 0.0 slice-start.2
  106.2 1.7 fusion.30
  107.9 0.0 slice-start.3
  107.9 0.0 slice-start.4
  108.0 0.0 copy-start.4
  108.0 3.4 fusion.41
  111.4 0.0 copy-start.6
  111.4 0.0 copy-start
  111.4 1.6 multiply_reduce_fusion
  113.0 1.1 multiply_convert_fusion.1
  114.1 0.0 all-gather.10.cloned.1.call-update
  114.1 0.0 all-gather.14.cloned.1.call-start
  114.2 0.5 all-gather.14.cloned.1.call-update
  114.7 0.0 reduce-scatter.2.cloned.1.call-start
  114.8 0.1 collective-permute-start
  114.9 43.5 %collective-permute-done = bf16[768,1024]{1,0:T(8,128)(2,1)} collective-permute-done((bf16[768,1024]{1,0:T(8,128)(2,1)S(1)}, bf16[768,1024]{1,0:T(8,128)(2,1)}, u32[]{:S(2)}, u32[]{:S(2)}) %collective-permute-start) | collective-permute-done | bytes 1572896 | tf_op jit(solution)/shard_map/ppermute | solution.py:18
  158.3 0.0 collective-permute-start.1
  158.3 1.7 collective-permute-start.2
  160.1 34.9 %collective-permute-done.1 = bf16[768,1024]{1,0:T(8,128)(2,1)} collective-permute-done((bf16[768,1024]{1,0:T(8,128)(2,1)}, bf16[768,1024]{1,0:T(8,128)(2,1)}, u32[]{:S(2)}, u32[]{:S(2)}) %collective-permute-start.1) | collective-permute-done | bytes 1572896 | tf_op jit(solution)/shard_map/ppermute | solution.py:18
  195.0 2.7 constant_dynamic-update-slice_fusion.7
  197.7 2.7 constant_dynamic-update-slice_fusion.6
  200.4 1.3 constant_dynamic-update-slice_fusion.5
  201.6 0.0 collective-permute-done.2
  201.6 2.7 constant_dynamic-update-slice_fusion.4
  204.4 2.7 constant_dynamic-update-slice_fusion.3
  207.0 2.8 constant_dynamic-update-slice_fusion.2
  209.8 1.3 constant_dynamic-update-slice_fusion.1
  211.1 2.7 constant_dynamic-update-slice_fusion
  213.8 43.0 %all-gather.10.cloned.1.call-done = bf16[1024,3072]{1,0:T(8,128)(2,1)} async-done(((bf16[128,3072]{1,0:T(8,128)(2,1)}), bf16[1024,3072]{1,0:T(8,128)(2,1)}) %all-gather.10.cloned.1.call-update) | async-done | bytes 6291472 | tf_op jit(solution)/shard_map/all_gather | solution.py:116
  256.8 11.3 %fusion.66 = f32[1024,1024]{1,0:T(8,128)S(1)} fusion(bf16[1024,3072]{1,0:T(8,128)(2,1)} %all-gather.10.cloned.1.call-done, bf16[3072,1024]{1,0:T(8,128)(2,1)} %all-gather.12.cloned.1.call-done), kind=kOutput, calls=%fused_computation.82 | convolution fusion | flops 6442450944 | bytes 16777216 | tf_op jit(solution)/shard_map/dot_general | solution.py:119
  268.0 0.0 copy-done.7
  268.1 10.3 %multiply_convert_fusion = bf16[1024,1024]{1,0:T(8,128)(2,1)} fusion(f32[1024,1024]{1,0:T(8,128)S(1)} %fusion.66, bf16[1024,3072]{1,0:T(8,128)(2,1)S(1)} %copy-done.7, bf16[6144,1024]{1,0:T(8,128)(2,1)} %constant_dynamic-update-slice_fusion, s32[]{:T(128)S(6)} %select_n.69), kind=kOutput, calls=%fused_computation.18 | convolution fusion | flops 6448742400 | bytes 18874372 | tf_op jit(solution)/shard_map/dot_general | solution.py:119
  278.4 24.4 %all-gather.14.cloned.1.call-done = bf16[1024,3072]{1,0:T(8,128)(2,1)} async-done(((bf16[1024,768]{1,0:T(8,128)(2,1)}), bf16[1024,3072]{1,0:T(8,128)(2,1)}) %all-gather.14.cloned.1.call-update) | async-done | bytes 6291472 | tf_op jit(solution)/shard_map/all_gather | solution.py:126
  302.8 11.2 %convolution_convert_fusion = bf16[1024,3072]{1,0:T(8,128)(2,1)} fusion(bf16[1024,1024]{1,0:T(8,128)(2,1)} %multiply_convert_fusion, bf16[1024,3072]{1,0:T(8,128)(2,1)} %all-gather.14.cloned.1.call-done), kind=kOutput, calls=%fused_computation.14 | convolution fusion | flops 6445596672 | bytes 14680064 | tf_op jit(solution)/shard_map/dot_general | solution.py:124
  314.0 0.0 reduce-scatter.2.cloned.1.call-update
  314.0 118.1 %reduce-scatter.2.cloned.1.call-done = bf16[128,3072]{1,0:T(8,128)(2,1)} async-done(((bf16[1024,3072]{1,0:T(8,128)(2,1)}), bf16[128,3072]{1,0:T(8,128)(2,1)}) %reduce-scatter.2.cloned.1.call-update) | async-done | bytes 786448 | tf_op jit(solution)/shard_map/reduce_scatter | solution.py:129
  432.2 2.2 add_convert_fusion
  (25 shorter events, 0.1 us)
Async XLA Ops:
  6.5 74.2 %all-gather.6.cloned.1.call-start = ((), (), s32[]{:S(2)}) async-start(), calls=%async_computation.1 | async-start | bytes 1179648 | tf_op jit(solution)/shard_map/all_gather | solution.py:90
  7.3 89.1 %all-gather.8.cloned.1.call-start = ((), (), s32[]{:S(2)}) async-start(), calls=%async_computation.2 | async-start | bytes 1179648 | tf_op jit(solution)/shard_map/all_gather | solution.py:91
  8.0 205.8 %all-gather.12.cloned.1.call-start = ((), (), s32[]{:S(2)}) async-start(), calls=%async_computation.4 | async-start | bytes 7864320 | tf_op jit(solution)/shard_map/all_gather | solution.py:121
  8.7 248.0 %all-gather.10.cloned.1.call-start = ((), (), s32[]{:S(2)}) async-start(), calls=%async_computation.3 | async-start | bytes 7077888 | tf_op jit(solution)/shard_map/all_gather | solution.py:116
  48.9 28.1 %copy-start.1 = (pred[128,1024]{0,1:T(8,128)(4,1)}, pred[128,1024]{0,1:T(8,128)(4,1)S(1)}, u32[]{:S(2)}) copy-start(pred[128,1024]{0,1:T(8,128)(4,1)S(1)} %fusion.46) | copy-start | bytes 393220
  96.3 4.3 slice-start
  98.7 2.2 slice-start.1
  98.7 2.2 copy-start.2
  102.4 3.8 copy-start.5
  106.2 1.7 copy-start.3
  106.2 5.1 %slice-start.2 = ((s8[9437184]{0:T(1024)(128)(4,1)}), s8[4194304]{0:T(1024)(128)(4,1)S(1)}, s32[]{:S(2)}) async-start(s8[9437184]{0:T(1024)(128)(4,1)} %bitcast.104), calls=%async_computation.9 | async-start | bytes 8388608
  107.9 3.4 slice-start.3
  107.9 3.4 slice-start.4
  108.0 3.4 copy-start.4
  111.4 1.6 copy-start.6
  111.4 3.4 copy-start
  114.1 188.6 %all-gather.14.cloned.1.call-start = ((), (), s32[]{:S(2)}) async-start(), calls=%async_computation.5 | async-start | bytes 7864320 | tf_op jit(solution)/shard_map/all_gather | solution.py:126
  114.7 317.4 %reduce-scatter.2.cloned.1.call-start = ((), (), s32[]{:S(2)}) async-start(), calls=%async_computation.6 | async-start | bytes 7077888 | tf_op jit(solution)/shard_map/reduce_scatter | solution.py:129
  114.8 43.5 %collective-permute-start = (bf16[768,1024]{1,0:T(8,128)(2,1)S(1)}, bf16[768,1024]{1,0:T(8,128)(2,1)}, u32[]{:S(2)}, u32[]{:S(2)}) collective-permute-start(bf16[768,1024]{1,0:T(8,128)(2,1)S(1)} %copy-done), channel_id=1, source_target_pairs={{0,8},{8,16},{16,24},{24,0},{1,9},{9,17},{17,25},{25,1},{2,10},{10... | collective-permute-start | bytes 4718600 | tf_op jit(solution)/shard_map/ppermute | solution.py:18
  158.3 36.7 %collective-permute-start.1 = (bf16[768,1024]{1,0:T(8,128)(2,1)}, bf16[768,1024]{1,0:T(8,128)(2,1)}, u32[]{:S(2)}, u32[]{:S(2)}) collective-permute-start(bf16[768,1024]{1,0:T(8,128)(2,1)} %collective-permute-done), channel_id=1, source_target_pairs={{0,8},{8,16},{16,24},{24,0},{1,9},{9,17},{17,25},{25,1},{2,10},{10... | collective-permute-start | bytes 4718600 | tf_op jit(solution)/shard_map/ppermute | solution.py:18
  158.3 43.3 %collective-permute-start.2 = (bf16[768,1024]{1,0:T(8,128)(2,1)S(1)}, bf16[768,1024]{1,0:T(8,128)(2,1)}, u32[]{:S(2)}, u32[]{:S(2)}) collective-permute-start(bf16[768,1024]{1,0:T(8,128)(2,1)S(1)} %copy-done), channel_id=1, source_target_pairs={{0,24},{8,0},{16,8},{24,16},{1,25},{9,1},{17,9},{25,17},{2,26},{10... | collective-permute-start | bytes 4718600 | tf_op jit(solution)/shard_map/ppermute | solution.py:20
  256.8 11.3 %copy-start.7 = (bf16[1024,3072]{1,0:T(8,128)(2,1)S(1)}, bf16[1024,3072]{1,0:T(8,128)(2,1)}, u32[]{:S(2)}) copy-start(bf16[1024,3072]{1,0:T(8,128)(2,1)} %all-gather.10.cloned.1.call-done) | copy-start | bytes 18874372
Sparse Core Ops, SparseCore 0:
  9.5 45.0 all-gather.5
  56.7 39.6 all-gather.7
  97.9 57.0 all-gather.11
  157.0 99.7 all-gather.9
  258.2 44.5 all-gather.13
  314.1 117.9 reduce-scatter.1
